TPU v7x, 256 devices: a whole 4x4x8 slice. The times are simulated.
256 devices in a mesh: seq: 32 (over x, y, core), head: 8 (over z).
Axes of the slice: x: 4, y: 4, z: 8, core: 2. Of those that a mesh axis runs over, the one named last changes fastest.
Arguments:
- tokens: bfloat16 [32768, 2048], P('seq'), may hold values from -6 to 6
- norm_gain: bfloat16 [2048], replicated, may hold values from 0.099609375 to 1.8984375
- w_qkv: bfloat16 [3, 2048, 2048], P(None, None, 'head'), may hold values from -0.176776695 to 0.176776695
- mem_gate: float32 [16], P('head'), may hold values from -3 to 3
- w_out: bfloat16 [2048, 2048], P('head'), may hold values from -0.1875 to 0.1875
Outputs:
- attended: bfloat16 [32768, 2048], P('seq', 'head')
- memory_state: float32 [32, 16, 128, 128], P('seq', 'head')
All inputs are finite; a program needn't handle non-finite values.
Results may differ from a plain program's by a relative error of at most 0.01.
The roundings to bfloat16 on the way count: a program that leaves them out, or rounds other values in their place, can miss the bound.
Values may be sent and summed in bfloat16 or wider, within the bound.
A program may use at most 64 MiB of HBM per device.

v0:
```python
import jax
import jax.numpy as jnp
from jax import lax
from jax.sharding import PartitionSpec as P

HDIM = 128


def sent_together(arrays, axis, dim, along):
    columns = [a.reshape(*a.shape[:along], -1) for a in arrays]
    both = jnp.concatenate(columns, axis=along)
    result, at, gathered = (lax.all_gather(both, axis, axis=dim, tiled=True), 0, [])
    for a, column in zip(arrays, columns):
        section = result[..., at : at + column.shape[along]]
        gathered.append(section.reshape(*section.shape[:along], *a.shape[along:]))
        at += column.shape[along]
    return tuple(gathered)


def elu_one(values_in):
    return jnp.where(values_in > 0, values_in + 1.0, jnp.exp(jnp.minimum(values_in, 0.0)))


def on_device(tokens, norm_gain, w_qkv, mem_gate, w_out):
    seg_len = tokens.shape[0]
    local_heads = w_qkv.shape[2] // HDIM
    float_tokens = tokens.astype(jnp.float32)
    normed = (
        float_tokens
        * lax.rsqrt(jnp.mean(float_tokens * float_tokens, axis=-1, keepdims=True) + 1e-05)
        * norm_gain.astype(jnp.float32)
    ).astype(jnp.bfloat16)
    projected = jnp.einsum("td,cdh->cth", normed, w_qkv, preferred_element_type=jnp.float32).astype(
        jnp.bfloat16
    )
    queries = projected[0].reshape(seg_len, local_heads, HDIM)
    key_rows = projected[1].reshape(seg_len, local_heads, HDIM)
    value_rows = projected[2].reshape(seg_len, local_heads, HDIM)
    sig_keys = elu_one(key_rows.astype(jnp.float32))
    memory_delta = jnp.einsum("thd,the->hde", sig_keys, value_rows.astype(jnp.float32))
    delta_norm = jnp.sum(sig_keys, axis=0)
    zero_memory = jnp.zeros_like(memory_delta)
    zero_norm = jnp.zeros_like(delta_norm)
    my_index = lax.axis_index("seq")
    pieces = tuple(
        (
            part.astype(jnp.float32)
            for part in sent_together(
                (memory_delta[None].astype(jnp.bfloat16), delta_norm[None].astype(jnp.bfloat16)),
                "seq",
                0,
                3,
            )
        )
    )
    row_count = pieces[0].shape[0]
    keep_rows = (jnp.arange(row_count, dtype=jnp.int32) < my_index).astype(jnp.float32)
    memory_prev = zero_memory + jnp.sum(pieces[0] * keep_rows[:, None, None, None], axis=0)
    norm_prev = zero_norm + jnp.sum(pieces[1] * keep_rows[:, None, None], axis=0)
    inv_sqrt = 1.0 / HDIM**0.5
    scores = (
        jnp.einsum("qhd,khd->hqk", queries, key_rows, preferred_element_type=jnp.float32) * inv_sqrt
    )
    row_ids = lax.broadcasted_iota(jnp.int32, (seg_len, seg_len), 0)
    col_ids = lax.broadcasted_iota(jnp.int32, (seg_len, seg_len), 1)
    scores = jnp.where((col_ids <= row_ids)[None], scores, -1e30)
    weights = jax.nn.softmax(scores, axis=-1).astype(jnp.bfloat16)
    local_out = jnp.einsum("hqk,khd->qhd", weights, value_rows, preferred_element_type=jnp.float32)
    sig_q = elu_one(queries.astype(jnp.float32))
    retrieved = jnp.einsum("thd,hde->the", sig_q, memory_prev)
    normalizer = 1.0 + jnp.einsum("thd,hd->th", sig_q, norm_prev)
    gate_share = jax.nn.sigmoid(mem_gate)[None, :, None]
    mixed_out = (
        gate_share * retrieved / normalizer[..., None] + (1.0 - gate_share) * local_out
    ).astype(jnp.bfloat16)
    mixed_out = mixed_out.reshape(seg_len, local_heads * HDIM)
    weight_cols = lax.all_to_all(w_out, "head", split_axis=1, concat_axis=0, tiled=True)
    attended = jnp.dot(
        lax.all_gather(mixed_out, "head", axis=1, tiled=True),
        weight_cols,
        preferred_element_type=jnp.float32,
    ).astype(jnp.bfloat16)
    memory_state = ((memory_prev + memory_delta) / seg_len)[None]
    return (attended, memory_state)


def solution(mesh):
    placed = (P("seq", None), P(), P(None, None, "head"), P("head"), P("head", None))
    return jax.shard_map(
        on_device,
        mesh=mesh,
        in_specs=placed,
        out_specs=(P("seq", "head"), P("seq", "head", None, None)),
        check_vma=False,
    )
```

profile of v0, /device:TPU:1, one launch (start us, length us, event | category | flops | bytes accessed | tf_op | source)
XLA Modules:
  0.0 170.5 jit_solution(17933472047963940664)
XLA Ops:
  7.2 0.0 copy-start
  7.2 0.0 copy-start.2
  7.2 0.0 all-gather.3.cloned.1.call-start
  7.2 0.0 copy-start.1
  7.2 3.2 %fusion.1 = f32[1024]{0:T(1024)S(1)} fusion(bf16[1024,2048]{1,0:T(8,128)(2,1)} %param.5), kind=kLoop, calls=%fused_computation.3 | loop fusion | flops 6290432 | bytes 4198400 | tf_op jit(solution)/shard_map/reduce_sum | solution.py:30
  10.5 0.0 copy-done.2
  10.5 0.0 copy-done
  10.5 1.1 copy-done.1
  11.6 3.9 %fusion.17 = bf16[3,1024,256]{1,2,0:T(8,128)(2,1)S(1)} fusion(bf16[3,2048,256]{2,1,0:T(8,128)(2,1)S(1)} %copy-done, bf16[1024,2048]{1,0:T(8,128)(2,1)S(1)} %copy-done.1, f32[2048]{0:T(1024)S(1)} %convert_element_type.76, f32[1024]{0:T(1024)S(1)} %add_rsqrt_fusion), kind=kOutput, calls=%fused_computation.30 | convolution fusion | flops 3230400512 | bytes 8925184 | tf_op jit(solution)/shard_map/td,cdh->cth/dot_general | solution.py:33
  15.5 0.0 copy-start.3
  15.5 1.2 fusion.58
  16.7 0.4 fusion.32
  17.0 2.1 %copy.44 = bf16[1024,2,128]{2,0,1:T(8,128)(2,1)} copy(bf16[1024,2,128]{0,2,1:T(8,128)(2,1)} %bitcast.59) | data formatting | bytes 1048576 | tf_op jit(solution)/shard_map/reshape;squeeze | solution.py:37
  19.1 1.6 fusion.27
  20.8 0.7 copy.46
  21.4 0.0 all-gather.3.cloned.1.call-update
  21.5 0.2 all-gather.5.cloned.1.call-start
  21.7 2.1 %copy.47 = bf16[1024,2,128]{2,0,1:T(8,128)(2,1)} copy(bf16[1024,2,128]{0,2,1:T(8,128)(2,1)} %bitcast.61) | data formatting | bytes 1048576 | tf_op jit(solution)/shard_map/reshape;squeeze | solution.py:36
  23.8 1.3 iota_compare_fusion
  25.0 0.0 copy-done.3
  25.1 8.2 %fusion.59 = (f32[2,1024]{1,0:T(2,128)S(1)}, f32[2,1024,1024]{1,2,0:T(8,128)}) fusion(pred[1024,1024]{0,1:T(8,128)(4,1)} %iota_compare_fusion, bf16[1024,2,128]{0,2,1:T(8,128)(2,1)} %bitcast.62, bf16[1024,2,128]{0,2,1:T(8,128)(2,1)} %bitcast.60), kind=kOutput, calls=%fused_computation.78 | convolution fusion | flops 545260544 | bytes 10493952 | tf_op jit(solution)/shard_map/sub | solution.py:67
  33.2 5.3 %fusion.24 = f32[1024,2,128]{0,2,1:T(8,128)} fusion(bf16[1024,2,128]{0,2,1:T(8,128)(2,1)} %bitcast.66, f32[2,1024,1024]{1,2,0:T(8,128)} %get-tuple-element.18, f32[2,1024]{1,0:T(2,128)S(1)} %get-tuple-element.17, f32[2]{0:T(128)S(1)} %get-tuple-element.12), kind=kOutput, calls=%fused_computation.36 | convolution fusion | flops 541327360 | bytes 9969672 | tf_op jit(solution)/shard_map/hqk,khd->qhd/dot_general | solution.py:68
  38.5 36.3 %all-gather.3.cloned.1.call-done = bf16[32,2,128,129]{2,1,3,0:T(2,128)(2,1)} async-done(((bf16[1,2,128,129]{2,1,3,0:T(2,128)(2,1)}), bf16[32,2,128,129]{2,1,3,0:T(2,128)(2,1)}) %all-gather.3.cloned.1.call-update) | async-done | bytes 2113552 | tf_op jit(solution)/shard_map/all_gather | solution.py:12
  74.8 0.8 fusion.48
  75.6 1.4 fusion.36
  77.0 3.9 %multiply_reduce_fusion = f32[2,128,128]{1,0,2:T(2,128)S(1)} fusion(f32[32]{0:T(128)S(1)} %compare_convert_fusion, bf16[32,2,128,129]{2,1,3,0:T(2,128)(2,1)} %all-gather.3.cloned.1.call-done), kind=kLoop, calls=%fused_computation.15 | loop fusion | flops 3112960 | bytes 2228352 | tf_op jit(solution)/shard_map/reduce_sum | solution.py:58
  80.9 2.7 %fusion.25 = bf16[1024,2,128]{0,2,1:T(8,128)(2,1)} fusion(f32[1024,2,128]{0,2,1:T(8,128)} %fusion.24, bf16[1024,2,128]{2,0,1:T(8,128)(2,1)} %copy.47, f32[1024,2]{0,1:T(2,128)S(1)} %fusion.49, f32[2]{0:T(128)S(1)} %get-tuple-element.13, f32[2,128,128]{1,0,2:T(2,128)S(1)} %multiply_reduce_fusion), kind=kOutput, calls=%fused_computation.37 | convolution fusion | flops 69468160 | bytes 2236424 | tf_op jit(solution)/shard_map/thd,hde->the/dot_general | solution.py:70
  83.6 0.0 all-gather.5.cloned.1.call-update
  83.6 2.3 %copy.52 = bf16[256,2048]{0,1:T(8,128)(2,1)} copy(bf16[256,2048]{1,0:T(8,128)(2,1)} %param.9) | data formatting | bytes 2097152 | tf_op args[4]
  85.9 46.3 %all_to_all.19 = bf16[256,8,256]{0,2,1:T(8,128)(2,1)} all-to-all(bf16[256,8,256]{0,2,1:T(8,128)(2,1)} %bitcast.58), channel_id=1, replica_groups=mesh['seq'=32,'head'=8] {'head'}, dimensions={1} | all-to-all | bytes 2097152 | tf_op jit(solution)/shard_map/all_to_all | solution.py:77
  132.2 2.3 %copy.53 = bf16[8,256,256]{2,1,0:T(8,128)(2,1)} copy(bf16[8,256,256]{1,2,0:T(8,128)(2,1)} %bitcast.57) | data formatting | bytes 2097152 | tf_op jit(solution)/shard_map/all_to_all | solution.py:77
  134.6 0.8 copy.55
  135.3 23.8 %all-gather.5.cloned.1.call-done = bf16[1024,2048]{0,1:T(8,128)(2,1)} async-done(((bf16[1024,256]{0,1:T(8,128)(2,1)}), bf16[1024,2048]{0,1:T(8,128)(2,1)}) %all-gather.5.cloned.1.call-update) | async-done | bytes 4194320 | tf_op jit(solution)/shard_map/all_gather | solution.py:79
  159.1 4.6 %convolution_convert_fusion = bf16[1024,256]{1,0:T(8,128)(2,1)} fusion(bf16[1024,2048]{0,1:T(8,128)(2,1)} %all-gather.5.cloned.1.call-done, bf16[2048,256]{1,0:T(8,128)(2,1)} %bitcast.63), kind=kOutput, calls=%fused_computation.38 | convolution fusion | flops 1074003968 | bytes 5767168 | tf_op jit(solution)/shard_map/dot_general | solution.py:78
  (9 shorter events, 0.1 us)
Async XLA Ops:
  7.2 3.3 %copy-start = (bf16[3,2048,256]{2,1,0:T(8,128)(2,1)S(1)}, bf16[3,2048,256]{2,1,0:T(8,128)(2,1)}, u32[]{:S(2)}) copy-start(bf16[3,2048,256]{2,1,0:T(8,128)(2,1)} %param.7) | copy-start | bytes 9437188
  7.2 3.3 %copy-start.2 = (bf16[2048]{0:T(1024)(128)(2,1)S(1)}, bf16[2048]{0:T(1024)(128)(2,1)}, u32[]{:S(2)}) copy-start(bf16[2048]{0:T(1024)(128)(2,1)} %param.6) | copy-start | bytes 12292
  7.2 67.6 %all-gather.3.cloned.1.call-start = ((), (), s32[]{:S(2)}) async-start(), calls=%async_computation.1 | async-start | bytes 2179584 | tf_op jit(solution)/shard_map/all_gather | solution.py:12
  7.2 4.4 %copy-start.1 = (bf16[1024,2048]{1,0:T(8,128)(2,1)S(1)}, bf16[1024,2048]{1,0:T(8,128)(2,1)}, u32[]{:S(2)}) copy-start(bf16[1024,2048]{1,0:T(8,128)(2,1)} %param.5) | copy-start | bytes 12582916
  15.5 9.6 %copy-start.3 = (f32[2]{0:T(128)S(1)}, f32[2]{0:T(128)}, u32[]{:S(2)}) copy-start(f32[2]{0:T(128)} %param.8) | copy-start | bytes 28
  21.5 137.7 %all-gather.5.cloned.1.call-start = ((), (), s32[]{:S(2)}) async-start(), calls=%async_computation.2 | async-start | bytes 4718592 | tf_op jit(solution)/shard_map/all_gather | solution.py:79
Sparse Core Ops, SparseCore 0:
  21.6 53.1 all-gather.2
  83.7 75.3 all-gather.4
where the time goes:
time: 171 us
  waiting for transfers between devices  60.1 us (35%)
  blocking collectives  46.3 us (27%)
  matrix products  27.6 us (16%)
  between operations  14.2 us (8%)
  local copies, waits for them, and re-layouts  12.4 us (7%)
  other arithmetic  9.68 us (6%)
    all_to_all x1, blocking collectives, on_device(): lax.all_to_all(w_out, 'head', split_axis=1, concat_axis=0, tiled=True)  46.3 us
    all_gather x1, waiting for transfers between devices, sent_together(): lax.all_gather(both, axis, axis=dim, tiled=True)  36.3 us
    all_gather x1, waiting for transfers between devices, on_device(): lax.all_gather(mixed_out, 'head', axis=1, tiled=True)  23.8 us
    sub x1, matrix products, on_device(): weights = jax.nn.softmax(scores, axis=-1).astype(jnp.bfloat16)  8.15 us
    dot_general x1, matrix products, on_device(): jnp.einsum('hqk,khd->qhd', weights, value_rows, preferred_element_type=jn...  5.3 us
    dot_general x1, matrix products, on_device(): jnp.dot(lax.all_gather(mixed_out, 'head', axis=1, tiled=True), weight_col...  4.57 us
    unnamed x10, local copies, waits for them, and re-layouts  4.15 us
    reduce_sum x1, other arithmetic, on_device(): jnp.sum(pieces[0] * keep_rows[:, None, None, None], axis=0)  3.93 us
  transfers between devices with their start and end apart: 2, of which 2 were waited for; matrix products, arithmetic and copies ran while one was open for 13% of the time, Pallas kernels for 0%

commit v1 on v0

--- a/solution.py
+++ b/solution.py
@@ -76,7 +76,9 @@
     mixed_out = mixed_out.reshape(seg_len, local_heads * HDIM)
     weight_cols = lax.all_to_all(w_out, "head", split_axis=1, concat_axis=0, tiled=True)
     attended = jnp.dot(
-        lax.all_gather(mixed_out, "head", axis=1, tiled=True),
+        jnp.concatenate(
+            lax.all_to_all(jnp.stack([mixed_out] * lax.axis_size("head")), "head", 0, 0), axis=1
+        ),
         weight_cols,
         preferred_element_type=jnp.float32,
     ).astype(jnp.bfloat16)

time: 171 us -> 205 us (1.20)
  waiting for transfers between devices: 60.1 us -> 119 us
  blocking collectives: 46.3 us -> 0 us
  starting transfers between devices: 0.26 us -> 15.9 us
  local copies, waits for them, and re-layouts: 12.4 us -> 17.7 us
    all_to_all x0 -> x2, waiting for transfers between devices: none -> 96.1 us  [the longest x1 96.1 us: on_device(): lax.all_to_all(jnp.stack([mixed_out] * lax.axis_size('head')), 'head', 0, 0)]
    all_to_all x1 -> x0, blocking collectives: 46.3 us -> none  [on_device(): lax.all_to_all(w_out, 'head', split_axis=1, concat_axis=0, tiled=True)]
    all_gather x1 -> x0, waiting for transfers between devices: 23.8 us -> none  [on_device(): lax.all_gather(mixed_out, 'head', axis=1, tiled=True)]
    all_to_all x0 -> x2, starting transfers between devices: none -> 15.9 us  [the longest x1 9.01 us: on_device(): lax.all_to_all(w_out, 'head', split_axis=1, concat_axis=0, tiled=True)]
    all_gather x1, waiting for transfers between devices: 36.3 us -> 22.6 us  [sent_together(): lax.all_gather(both, axis, axis=dim, tiled=True)]
    another operation x0 -> x2, local copies, waits for them, and re-layouts: none -> 5.32 us  [on_device(): jnp.stack([mixed_out] * lax.axis_size('head'))]
  transfers between devices with their start and end apart: 2 -> 3, of which waited for: 2 -> 2; matrix products, arithmetic and copies ran while one was open for 13% -> 16% of each run, Pallas kernels for 0% -> 0%
where the time goes in v1:
time: 205 us; the launch traced here: 204 us
  waiting for transfers between devices  119 us (58%)
  matrix products  27.6 us (13%)
  local copies, waits for them, and re-layouts  17.7 us (9%)
  starting transfers between devices  15.9 us (8%)
  between operations  14.1 us (7%)
  other arithmetic  9.73 us (5%)
    all_to_all x1, waiting for transfers between devices, on_device(): lax.all_to_all(jnp.stack([mixed_out] * lax.axis_size('head')), 'head', 0, 0)  96.1 us
    all_gather x1, waiting for transfers between devices, sent_together(): lax.all_gather(both, axis, axis=dim, tiled=True)  22.6 us
    all_to_all x1, starting transfers between devices, on_device(): lax.all_to_all(w_out, 'head', split_axis=1, concat_axis=0, tiled=True)  9.01 us
    sub x1, matrix products, on_device(): weights = jax.nn.softmax(scores, axis=-1).astype(jnp.bfloat16)  8.17 us
    all_to_all x1, starting transfers between devices, on_device(): lax.all_to_all(jnp.stack([mixed_out] * lax.axis_size('head')), 'head', 0, 0)  6.87 us
    dot_general x1, matrix products, on_device(): jnp.einsum('hqk,khd->qhd', weights, value_rows, preferred_element_type=jn...  5.37 us
    another operation x2, local copies, waits for them, and re-layouts, on_device(): jnp.stack([mixed_out] * lax.axis_size('head'))  5.32 us
    dot_general x1, matrix products, on_device(): jnp.dot(jnp.concatenate(lax.all_to_all(jnp.stack([mixed_out] * lax.axis_s...  4.53 us
  transfers between devices with their start and end apart: 3, of which 2 were waited for; matrix products, arithmetic and copies ran while one was open for 16% of the time, Pallas kernels for 0%

profile of v1, /device:TPU:1, one launch (start us, length us, event | category | flops | bytes accessed | tf_op | source)
XLA Modules:
  0.0 203.9 jit_solution(14127953281207876791)
XLA Ops:
  7.2 0.0 copy-start
  7.2 0.0 copy-start.2
  7.2 0.0 all-gather.2.cloned.1.call-start
  7.2 0.0 copy-start.1
  7.2 3.2 %fusion.1 = f32[1024]{0:T(1024)S(1)} fusion(bf16[1024,2048]{1,0:T(8,128)(2,1)} %param.5), kind=kLoop, calls=%fused_computation.3 | loop fusion | flops 6290432 | bytes 4198400 | tf_op jit(solution)/shard_map/reduce_sum | solution.py:30
  10.5 0.0 copy-done.2
  10.5 0.0 copy-done
  10.5 1.1 copy-done.1
  11.6 3.9 %fusion.19 = bf16[3,1024,256]{1,2,0:T(8,128)(2,1)S(1)} fusion(bf16[3,2048,256]{2,1,0:T(8,128)(2,1)S(1)} %copy-done, bf16[1024,2048]{1,0:T(8,128)(2,1)S(1)} %copy-done.1, f32[2048]{0:T(1024)S(1)} %convert_element_type.76, f32[1024]{0:T(1024)S(1)} %add_rsqrt_fusion), kind=kOutput, calls=%fused_computation.32 | convolution fusion | flops 3230400512 | bytes 8925184 | tf_op jit(solution)/shard_map/td,cdh->cth/dot_general | solution.py:33
  15.5 1.2 fusion.67
  16.7 0.4 fusion.40
  17.0 2.0 copy.39
  19.0 1.6 fusion.35
  20.7 0.0 copy-start.3
  20.7 0.7 copy.41
  21.4 0.0 all-gather.2.cloned.1.call-update
  21.4 2.3 %copy.48 = bf16[256,2048]{0,1:T(8,128)(2,1)} copy(bf16[256,2048]{1,0:T(8,128)(2,1)} %param.9) | data formatting | bytes 2097152 | tf_op args[4]
  23.7 2.3 %copy.49 = bf16[256,8,256]{2,0,1:T(8,128)(2,1)} copy(bf16[256,8,256]{0,2,1:T(8,128)(2,1)} %bitcast.67) | data formatting | bytes 2097152 | tf_op jit(solution)/shard_map/all_to_all | solution.py:77
  26.0 9.0 %all-to-all-start.1 = ((bf16[256,8,256]{2,0,1:T(8,128)(2,1)}), bf16[256,8,256]{2,0,1:T(8,128)(2,1)}, u32[]{:S(2)}, u32[]{:S(2)}) async-start(bf16[256,8,256]{2,0,1:T(8,128)(2,1)} %copy.49), calls=%async_computation.1 | async-start | bytes 2097152 | tf_op jit(solution)/shard_map/all_to_all | solution.py:77
  35.0 1.3 iota_compare_fusion
  36.4 0.0 copy-done.3
  36.4 8.2 %fusion.68 = (f32[2,1024]{1,0:T(2,128)S(1)}, f32[2,1024,1024]{1,2,0:T(8,128)}) fusion(pred[1024,1024]{0,1:T(8,128)(4,1)} %iota_compare_fusion, bf16[1024,2,128]{0,2,1:T(8,128)(2,1)} %bitcast.68, bf16[1024,2,128]{0,2,1:T(8,128)(2,1)} %bitcast.71), kind=kOutput, calls=%fused_computation.82 | convolution fusion | flops 545260544 | bytes 10493952 | tf_op jit(solution)/shard_map/sub | solution.py:67
  44.5 5.4 %fusion.29 = f32[1024,2,128]{0,2,1:T(8,128)} fusion(bf16[1024,2,128]{0,2,1:T(8,128)(2,1)} %bitcast.74, f32[2,1024,1024]{1,2,0:T(8,128)} %get-tuple-element.16, f32[2,1024]{1,0:T(2,128)S(1)} %get-tuple-element.15, f32[2]{0:T(128)S(1)} %get-tuple-element.10), kind=kOutput, calls=%fused_computation.39 | convolution fusion | flops 541327360 | bytes 9969672 | tf_op jit(solution)/shard_map/hqk,khd->qhd/dot_general | solution.py:68
  49.9 2.0 %copy.42 = bf16[1024,2,128]{2,0,1:T(8,128)(2,1)} copy(bf16[1024,2,128]{0,2,1:T(8,128)(2,1)} %bitcast.69) | data formatting | bytes 1048576 | tf_op jit(solution)/shard_map/reshape;squeeze | solution.py:36
  52.0 22.6 %all-gather.2.cloned.1.call-done = bf16[32,2,128,129]{2,1,3,0:T(2,128)(2,1)} async-done(((bf16[1,2,128,129]{2,1,3,0:T(2,128)(2,1)}), bf16[32,2,128,129]{2,1,3,0:T(2,128)(2,1)}) %all-gather.2.cloned.1.call-update) | async-done | bytes 2113552 | tf_op jit(solution)/shard_map/all_gather | solution.py:12
  74.6 0.8 fusion.57
  75.4 1.4 fusion.45
  76.9 3.9 %multiply_reduce_fusion = f32[2,128,128]{1,0,2:T(2,128)S(1)} fusion(f32[32]{0:T(128)S(1)} %compare_convert_fusion, bf16[32,2,128,129]{2,1,3,0:T(2,128)(2,1)} %all-gather.2.cloned.1.call-done), kind=kLoop, calls=%fused_computation.17 | loop fusion | flops 3112960 | bytes 2228352 | tf_op jit(solution)/shard_map/reduce_sum | solution.py:58
  80.8 2.6 %fusion.30 = bf16[1024,2,128]{0,2,1:T(8,128)(2,1)} fusion(f32[1024,2,128]{0,2,1:T(8,128)} %fusion.29, bf16[1024,2,128]{2,0,1:T(8,128)(2,1)} %copy.42, f32[1024,2]{0,1:T(2,128)S(1)} %fusion.58, f32[2]{0:T(128)S(1)} %get-tuple-element.11, f32[2,128,128]{1,0,2:T(2,128)S(1)} %multiply_reduce_fusion), kind=kOutput, calls=%fused_computation.40 | convolution fusion | flops 69468160 | bytes 2236424 | tf_op jit(solution)/shard_map/thd,hde->the/dot_general | solution.py:70
  83.4 2.0 %copy.47 = bf16[1024,256]{1,0:T(8,128)(2,1)} copy(bf16[1024,256]{0,1:T(8,128)(2,1)} %bitcast.72) | data formatting | bytes 1048576 | tf_op jit(solution)/shard_map/stack;reshape | solution.py:80
  85.5 0.0 all-to-all-done.1
  85.5 3.3 %stack.3 = bf16[8,1024,256]{2,1,0:T(8,128)(2,1)} broadcast(bf16[1024,256]{1,0:T(8,128)(2,1)} %copy.47), dimensions={1,2} | broadcast | bytes 4718592 | tf_op jit(solution)/shard_map/stack | solution.py:80
  88.8 6.9 %all-to-all-start = ((bf16[8,1024,256]{2,1,0:T(8,128)(2,1)}), bf16[8,1024,256]{2,1,0:T(8,128)(2,1)}, u32[]{:S(2)}, u32[]{:S(2)}) async-start(bf16[8,1024,256]{2,1,0:T(8,128)(2,1)} %stack.3), calls=%async_computation | async-start | bytes 8388608 | tf_op jit(solution)/shard_map/all_to_all | solution.py:80
  95.7 0.8 copy.51
  96.4 96.1 %all-to-all-done = bf16[8,1024,256]{2,1,0:T(8,128)(2,1)} async-done(((bf16[8,1024,256]{2,1,0:T(8,128)(2,1)}), bf16[8,1024,256]{2,1,0:T(8,128)(2,1)}, u32[]{:S(2)}, u32[]{:S(2)}) %all-to-all-start) | async-done | bytes 4194336 | tf_op jit(solution)/shard_map/all_to_all | solution.py:80
  192.5 4.5 %fusion.31 = bf16[1024,256]{1,0:T(8,128)(2,1)} fusion(bf16[8,1024,256]{2,1,0:T(8,128)(2,1)} %all-to-all-done, bf16[256,8,256]{2,0,1:T(8,128)(2,1)} %all-to-all-done.1), kind=kOutput, calls=%fused_computation.41 | convolution fusion | flops 1074003968 | bytes 5767168 | tf_op jit(solution)/shard_map/dot_general | solution.py:78
  (9 shorter events, 0.1 us)
Async XLA Ops:
  7.2 3.3 %copy-start = (bf16[3,2048,256]{2,1,0:T(8,128)(2,1)S(1)}, bf16[3,2048,256]{2,1,0:T(8,128)(2,1)}, u32[]{:S(2)}) copy-start(bf16[3,2048,256]{2,1,0:T(8,128)(2,1)} %param.7) | copy-start | bytes 9437188
  7.2 3.3 %copy-start.2 = (bf16[2048]{0:T(1024)(128)(2,1)S(1)}, bf16[2048]{0:T(1024)(128)(2,1)}, u32[]{:S(2)}) copy-start(bf16[2048]{0:T(1024)(128)(2,1)} %param.6) | copy-start | bytes 12292
  7.2 67.4 %all-gather.2.cloned.1.call-start = ((), (), s32[]{:S(2)}) async-start(), calls=%async_computation.2 | async-start | bytes 2179584 | tf_op jit(solution)/shard_map/all_gather | solution.py:12
  7.2 4.4 %copy-start.1 = (bf16[1024,2048]{1,0:T(8,128)(2,1)S(1)}, bf16[1024,2048]{1,0:T(8,128)(2,1)}, u32[]{:S(2)}) copy-start(bf16[1024,2048]{1,0:T(8,128)(2,1)} %param.5) | copy-start | bytes 12582916
  20.7 15.7 %copy-start.3 = (f32[2]{0:T(128)S(1)}, f32[2]{0:T(128)}, u32[]{:S(2)}) copy-start(f32[2]{0:T(128)} %param.8) | copy-start | bytes 28
  26.0 59.5 %all-to-all-start.1 = ((bf16[256,8,256]{2,0,1:T(8,128)(2,1)}), bf16[256,8,256]{2,0,1:T(8,128)(2,1)}, u32[]{:S(2)}, u32[]{:S(2)}) async-start(bf16[256,8,256]{2,0,1:T(8,128)(2,1)} %copy.49), calls=%async_computation.1 | async-start | bytes 2097152 | tf_op jit(solution)/shard_map/all_to_all | solution.py:77
  88.8 103.7 %all-to-all-start = ((bf16[8,1024,256]{2,1,0:T(8,128)(2,1)}), bf16[8,1024,256]{2,1,0:T(8,128)(2,1)}, u32[]{:S(2)}, u32[]{:S(2)}) async-start(bf16[8,1024,256]{2,1,0:T(8,128)(2,1)} %stack.3), calls=%async_computation | async-start | bytes 8388608 | tf_op jit(solution)/shard_map/all_to_all | solution.py:80
Sparse Core Ops, SparseCore 0:
  21.6 52.9 all-gather.1
